TPU v7x, 32 devices: a whole 2x2x4 slice. The times are simulated.
32 devices in a mesh: store: 8 (over z, y), tensor: 4 (over x, core).
Axes of the slice: x: 2, y: 2, z: 4, core: 2. Of those that a mesh axis runs over, the one named last changes fastest.
Arguments:
- tokens: bfloat16 [8192, 8192], P('store', 'tensor'), may hold values from -1200 to 1200
- norm_gain: float32 [8192], P('tensor'), may hold values from 0.1 to 1.9
- kv_weight: bfloat16 [8192, 2, 1024], P('tensor'), may hold values from -0.0625 to 0.0625
- adapter_down: bfloat16 [32, 8192, 128], P('store', 'tensor'), may hold values from -0.0625 to 0.0625
- adapter_up: bfloat16 [32, 2, 64, 1024], P('store', None, None, 'tensor'), may hold values from -0.75 to 0.75
- token_adapters: int32 [8192, 1], P('store'), may hold values from 0 to 31; in each aligned block of 1024 rows (0 to 1023, 1024 to 2047, ...) at most 40 rows name the same one
- adapter_slot: int32 [32], replicated, may hold values from 0 to 31, each once
- request_lengths: int32 [16], replicated, may hold values from 1 to 4096, 8192 in all
Outputs:
- new_keys: bfloat16 [8192, 1024], P('store', 'tensor')
- new_values: bfloat16 [8192, 1024], P('store', 'tensor')
Inputs may be any that keep to these rules, and one draw needn't show every extreme that they name: `token_adapters`: among the 1024 tokens of one index of store no adapter is named more than 40 times; in every draw some adapter is named exactly 40 times by the tokens of some index. `adapter_slot`: each row 0 to 31 appears once. `request_lengths`: the lengths sum to 8192; the largest is exactly 4096.
All inputs are finite; a program needn't handle non-finite values.
Results may differ from a plain program's by a relative error of at most 0.0061.
Values may be sent and summed in bfloat16 or wider, within the bound.
A program may use at most 128 MiB of HBM per device.

v0:
```python
import math
import jax
import jax.numpy as jnp
from jax import lax
from jax.sharding import PartitionSpec as P

D = 8192
HEAD = 128
ADAPTER_RANK = 64
epsilon = 1e-05
adapter_scale = 2.0
rope_theta = 500000.0


def place_rows(adapter_ids, adapter_slot, capacity):
    catalog = jnp.arange(adapter_slot.shape[0], dtype=jnp.int32)
    slot_rows = jnp.sum(
        jnp.where(adapter_ids[:, None] == catalog[None, :], adapter_slot[None, :], 0), axis=1
    )
    row_order = jnp.arange(adapter_ids.shape[0], dtype=jnp.int32)
    same_earlier = (adapter_ids[:, None] == adapter_ids[None, :]) & (
        row_order[None, :] < row_order[:, None]
    )
    rank_rows = jnp.sum(same_earlier.astype(jnp.int32), axis=1)
    return slot_rows * capacity + rank_rows


def positions_of(first_row, row_count, lengths):
    global_rows = first_row + jnp.arange(row_count, dtype=jnp.int32)
    request_ends = jnp.cumsum(lengths)
    preceding = jnp.sum(
        jnp.where(request_ends[None, :] <= global_rows[:, None], lengths[None, :], 0), axis=1
    )
    return global_rows - preceding


def rotate(states, positions):
    per_head = states.reshape(states.shape[0], -1, HEAD)
    half_size = HEAD // 2
    frequency = jnp.exp(
        jnp.arange(half_size, dtype=jnp.float32) * (-2.0 * math.log(rope_theta) / HEAD)
    )
    angles = positions.astype(jnp.float32)[:, None] * frequency[None, :]
    cos_part = jnp.concatenate([jnp.cos(angles), jnp.cos(angles)], axis=1)[:, None, :]
    sin_part = jnp.concatenate([jnp.sin(angles), jnp.sin(angles)], axis=1)[:, None, :]
    low_half = per_head[..., :half_size]
    high_half = per_head[..., half_size:]
    turned = jnp.concatenate([-high_half, low_half], axis=-1)
    return (per_head * cos_part + turned * sin_part).reshape(states.shape)


def local(
    tokens,
    norm_gain,
    kv_weight,
    adapter_down,
    adapter_up,
    token_adapters,
    adapter_slot,
    request_lengths,
):
    row_count = tokens.shape[0]
    local_width = tokens.shape[1]
    adapter_total = adapter_slot.shape[0]
    capacity = max(2, 5 * row_count // (4 * adapter_total))
    store_size = lax.axis_size("store")
    per_owner = adapter_down.shape[0]
    kv_local = adapter_up.shape[3]
    widened = tokens.astype(jnp.float32)
    squares = lax.psum(jnp.sum(widened * widened, axis=1), "tensor")
    normed = (widened * lax.rsqrt(squares / D + epsilon)[:, None] * norm_gain[None, :]).astype(
        jnp.bfloat16
    )
    targets = place_rows(token_adapters[:, 0], adapter_slot, capacity)
    send_rows = (
        jnp.zeros((adapter_total * capacity, local_width), jnp.bfloat16).at[targets].set(normed)
    )
    send_rows = send_rows.reshape(store_size, per_owner, capacity, local_width)
    down_projected = jnp.einsum(
        "slcd,ldr->slcr",
        lax.all_to_all(send_rows, "store", split_axis=0, concat_axis=0, tiled=True),
        adapter_down,
        preferred_element_type=jnp.float32,
    )
    rank_total_sum = lax.psum(down_projected, "tensor")
    rank_activation = (rank_total_sum * adapter_scale).astype(jnp.bfloat16)
    split_rank = rank_activation.reshape(rank_activation.shape[:3] + (2, ADAPTER_RANK))
    update_rows = jnp.einsum(
        "slcjr,ljrk->slcjk", split_rank, adapter_up, preferred_element_type=jnp.float32
    )
    back_rows = update_rows.astype(jnp.bfloat16).reshape(
        rank_activation.shape[:3] + (2 * kv_local,)
    )
    returned = lax.all_to_all(back_rows, "store", split_axis=0, concat_axis=0, tiled=True)
    delta_rows = returned.reshape(adapter_total * capacity, 2, kv_local)[targets]
    partial_value = jnp.einsum("td,djk->tjk", normed, kv_weight, preferred_element_type=jnp.float32)
    base_part = lax.psum_scatter(partial_value, "tensor", scatter_dimension=2, tiled=True)
    combined = base_part + delta_rows.astype(jnp.float32)
    positions = positions_of(lax.axis_index("store") * row_count, row_count, request_lengths)
    new_keys = rotate(combined[:, 0, :], positions).astype(jnp.bfloat16)
    new_values = combined[:, 1, :].astype(jnp.bfloat16)
    return (new_keys, new_values)


def solution(mesh):
    return jax.shard_map(
        local,
        mesh=mesh,
        in_specs=(
            P("store", "tensor"),
            P("tensor"),
            P("tensor", None, None),
            P("store", "tensor", None),
            P("store", None, None, "tensor"),
            P("store", None),
            P(),
            P(),
        ),
        out_specs=(P("store", "tensor"), P("store", "tensor")),
        check_vma=False,
    )
```

profile of v0, /device:TPU:0, one launch (start us, length us, event | category | flops | bytes accessed | tf_op | source)
XLA Modules:
  0.0 278.7 jit_solution(12801032871038219586)
XLA Ops:
  7.2 1.4 convert_reduce_fusion
  9.4 3.1 %fusion = f32[1024]{0:T(1024)S(1)} fusion(bf16[1024,2048]{1,0:T(8,128)(2,1)} %param.8), kind=kLoop, calls=%fused_computation.4 | loop fusion | flops 6290432 | bytes 4198400 | tf_op jit(solution)/shard_map/reduce_sum | solution.py:70
  12.5 8.4 %psum.14 = f32[1024]{0:T(1024)S(1)} all-reduce(f32[1024]{0:T(1024)S(1)} %fusion), channel_id=1, replica_groups=mesh['store'=8,'tensor'=4] {'tensor'}, use_global_device_ids=true, to_apply=%region_1.0 | all-reduce | flops 1024 | bytes 8192 | tf_op jit(solution)/shard_map/psum | solution.py:70
  20.9 11.2 %scatter_custom_fusion = bf16[1280,2048]{1,0:T(8,128)(2,1)} fusion(s32[1024]{0:T(1024)S(1)} %bitcast.50, bf16[]{:T(256)} %constant.6.clone.1, bf16[1024,2048]{1,0:T(8,128)(2,1)} %param.8, f32[2048]{0:T(1024)S(1)} %copy-done.6, f32[1024]{0:T(1024)S(1)} %add_rsqrt_fusion), kind=kCustom, calls=%fused_computation.15 | custom fusion | flops 8388608 | bytes 9449474 | tf_op jit(solution)/shard_map/scatter | solution.py:76
  32.1 120.3 %all_to_all.10 = bf16[8,4,40,2048]{3,2,1,0:T(8,128)(2,1)S(1)} all-to-all(bf16[8,4,40,2048]{3,2,1,0:T(8,128)(2,1)} %bitcast.46), channel_id=1, replica_groups=mesh['store'=8,'tensor'=4] {'store'}, dimensions={0} | all-to-all | bytes 10485760 | tf_op jit(solution)/shard_map/all_to_all | solution.py:81
  152.4 2.5 fusion.13
  155.1 14.9 %fusion.3 = f32[1024,2,1024]{2,0,1:T(8,128)} fusion(bf16[2048,2,1024]{2,1,0:T(2,128)(2,1)} %param.10, bf16[1024,2048]{1,0:T(8,128)(2,1)} %param.8, f32[2048]{0:T(1024)S(1)} %copy-done.6, f32[1024]{0:T(1024)S(1)} %add_rsqrt_fusion), kind=kOutput, calls=%fused_computation.7 | convolution fusion | flops 8598323200 | bytes 20983808 | tf_op jit(solution)/shard_map/td,djk->tjk/dot_general | solution.py:96
  170.0 18.1 %all-reduce.2.cloned.1.call-done = f32[8,4,40,128]{3,2,0,1:T(8,128)} async-done(((f32[8,4,40,128]{3,2,0,1:T(8,128)}), f32[8,4,40,128]{3,2,0,1:T(8,128)}) %all-reduce.2.cloned.1.call-update) | async-done | bytes 655376 | tf_op jit(solution)/shard_map/psum | solution.py:85
  188.1 1.1 multiply_convert_fusion
  190.1 1.3 copy.28
  191.5 1.7 reshape.97
  193.2 5.5 %all-to-all-start.1 = ((bf16[8,4,40,512]{3,2,1,0:T(8,128)(2,1)}), bf16[8,4,40,512]{3,2,1,0:T(8,128)(2,1)S(1)}, u32[]{:S(2)}, u32[]{:S(2)}) async-start(bf16[8,4,40,512]{3,2,1,0:T(8,128)(2,1)} %reshape.97), calls=%async_computation.2 | async-start | bytes 2621440 | tf_op jit(solution)/shard_map/all_to_all | solution.py:94
  199.0 1.9 multiply_cosine_fusion
  200.9 1.3 pad_maximum_fusion
  202.2 27.2 %all-to-all-done.1 = bf16[8,4,40,512]{3,2,1,0:T(8,128)(2,1)S(1)} async-done(((bf16[8,4,40,512]{3,2,1,0:T(8,128)(2,1)}), bf16[8,4,40,512]{3,2,1,0:T(8,128)(2,1)S(1)}, u32[]{:S(2)}, u32[]{:S(2)}) %all-to-all-start.1) | async-done | bytes 1310752 | tf_op jit(solution)/shard_map/all_to_all | solution.py:94
  229.4 1.2 reshape.98
  230.6 5.5 %gather_fusion = bf16[1024,2,256]{2,1,0:T(2,128)(2,1)S(1)} fusion(bf16[1280,2,256]{2,1,0:T(2,128)(2,1)} %reshape.98, s32[1024]{0:T(1024)S(1)} %broadcast_clamp_fusion), kind=kCustom, calls=%fused_computation | custom fusion | bytes 2101248 | tf_op jit(solution)/shard_map/gather | solution.py:95
  236.1 25.9 %reduce-scatter.2.cloned.1.call-done = f32[1024,2,256]{2,0,1:T(8,128)} async-done(((f32[1024,2,1024]{2,0,1:T(8,128)}), f32[1024,2,256]{2,0,1:T(8,128)}) %reduce-scatter.2.cloned.1.call-update) | async-done | bytes 2097168 | tf_op jit(solution)/shard_map/reduce_scatter | solution.py:97
  262.0 1.8 convert_add_fusion
  263.8 1.1 slice.19
  266.3 1.7 reshape_squeeze.6
  268.1 1.1 slice_negate_fusion
  269.3 1.2 maximum_multiply_fusion
  270.9 1.0 fusion.20
  (36 shorter events, 4.0 us)
Async XLA Ops:
  7.2 145.2 %copy-start = (bf16[4,2048,128]{2,1,0:T(8,128)(2,1)S(1)}, bf16[4,2048,128]{2,1,0:T(8,128)(2,1)}, u32[]{:S(2)}) copy-start(bf16[4,2048,128]{2,1,0:T(8,128)(2,1)} %param.11) | copy-start | bytes 6291460
  7.2 13.7 %copy-start.6 = (f32[2048]{0:T(1024)S(1)}, f32[2048]{0:T(1024)}, u32[]{:S(2)}) copy-start(f32[2048]{0:T(1024)} %param.9) | copy-start | bytes 24580
  7.2 180.9 %all-reduce.2.cloned.1.call-start = ((), (), s32[]{:S(2)}) async-start(), calls=%async_computation.4 | async-start | bytes 1310720 | tf_op jit(solution)/shard_map/psum | solution.py:85
  154.9 107.1 %reduce-scatter.2.cloned.1.call-start = ((), (), s32[]{:S(2)}) async-start(), calls=%async_computation.3 | async-start | bytes 10485760 | tf_op jit(solution)/shard_map/reduce_scatter | solution.py:97
  170.0 19.6 %copy-start.5 = (bf16[4,2,64,256]{3,2,1,0:T(8,128)(2,1)S(1)}, bf16[4,2,64,256]{3,2,1,0:T(8,128)(2,1)}, u32[]{:S(2)}) copy-start(bf16[4,2,64,256]{3,2,1,0:T(8,128)(2,1)} %param.12) | copy-start | bytes 786436
  190.1 8.6 %copy-start.7 = (s32[16]{0:T(128)S(1)}, s32[16]{0:T(128)}, u32[]{:S(2)}) copy-start(s32[16]{0:T(128)} %param.15) | copy-start | bytes 196
  193.2 36.3 %all-to-all-start.1 = ((bf16[8,4,40,512]{3,2,1,0:T(8,128)(2,1)}), bf16[8,4,40,512]{3,2,1,0:T(8,128)(2,1)S(1)}, u32[]{:S(2)}, u32[]{:S(2)}) async-start(bf16[8,4,40,512]{3,2,1,0:T(8,128)(2,1)} %reshape.97), calls=%async_computation.2 | async-start | bytes 2621440 | tf_op jit(solution)/shard_map/all_to_all | solution.py:94
  263.8 1.7 copy-start.1
  268.1 1.2 copy-start.4
  268.1 2.4 copy-start.3
  268.1 2.8 copy-start.2
Sparse Core Ops, SparseCore 0:
  155.0 33.0 all-reduce.1
  190.7 71.2 reduce-scatter.1
where the time goes:
time: 279 us
  blocking collectives  129 us (46%)
  waiting for transfers between devices  71.1 us (25%)
  other arithmetic  26.2 us (9%)
  matrix products  17.9 us (6%)
  local copies, waits for them, and re-layouts  14.8 us (5%)
  between operations  14.2 us (5%)
  starting transfers between devices  5.78 us (2%)
    all_to_all x1, blocking collectives, local(): lax.all_to_all(send_rows, 'store', split_axis=0, concat_axis=0, tiled=True)  120 us
    all_to_all x1, waiting for transfers between devices, local(): lax.all_to_all(back_rows, 'store', split_axis=0, concat_axis=0, tiled=True)  27.2 us
    reduce_scatter x1, waiting for transfers between devices, local(): lax.psum_scatter(partial_value, 'tensor', scatter_dimension=2, tiled=True)  25.9 us
    psum x1, waiting for transfers between devices, local(): rank_total_sum = lax.psum(down_projected, 'tensor')  18.1 us
    dot_general x1, matrix products, local(): jnp.einsum('td,djk->tjk', normed, kv_weight, preferred_element_type=jnp.f...  14.9 us
    scatter x1, other arithmetic, local(): jnp.zeros((adapter_total * capacity, local_width), jnp.bfloat16).at[targets]  11.2 us
    psum x1, blocking collectives, local(): squares = lax.psum(jnp.sum(widened * widened, axis=1), 'tensor')  8.38 us
  transfers between devices with their start and end apart: 3, of which 3 were waited for; matrix products, arithmetic and copies ran while one was open for 11% of the time, Pallas kernels for 0%

commit v1 on v0

--- a/solution.py
+++ b/solution.py
@@ -82,7 +82,7 @@
         adapter_down,
         preferred_element_type=jnp.float32,
     )
-    rank_total_sum = lax.psum(down_projected, "tensor")
+    rank_total_sum = jnp.sum(lax.all_gather(down_projected, "tensor"), axis=0)
     rank_activation = (rank_total_sum * adapter_scale).astype(jnp.bfloat16)
     split_rank = rank_activation.reshape(rank_activation.shape[:3] + (2, ADAPTER_RANK))
     update_rows = jnp.einsum(

time: 279 us -> 271 us (0.971)
  waiting for transfers between devices: 71.1 us -> 61.6 us
    psum x1 -> x0, waiting for transfers between devices: 18.1 us -> none  [local(): rank_total_sum = lax.psum(down_projected, 'tensor')]
    all_gather x0 -> x1, waiting for transfers between devices: none -> 9.57 us  [local(): rank_total_sum = jnp.sum(lax.all_gather(down_projected, 'tensor'), axis=0)]
  transfers between devices with their start and end apart: 3 -> 3, of which waited for: 3 -> 3; matrix products, arithmetic and copies ran while one was open for 11% -> 12% of each run, Pallas kernels for 0% -> 0%
where the time goes in v1:
time: 271 us; the launch traced here: 270 us
  blocking collectives  129 us (48%)
  waiting for transfers between devices  61.6 us (23%)
  other arithmetic  27.1 us (10%)
  matrix products  17.9 us (7%)
  local copies, waits for them, and re-layouts  14.9 us (5%)
  between operations  14.3 us (5%)
  starting transfers between devices  5.78 us (2%)
    all_to_all x1, blocking collectives, local(): lax.all_to_all(send_rows, 'store', split_axis=0, concat_axis=0, tiled=True)  120 us
    all_to_all x1, waiting for transfers between devices, local(): lax.all_to_all(back_rows, 'store', split_axis=0, concat_axis=0, tiled=True)  28.2 us
    reduce_scatter x1, waiting for transfers between devices, local(): lax.psum_scatter(partial_value, 'tensor', scatter_dimension=2, tiled=True)  23.8 us
    dot_general x1, matrix products, local(): jnp.einsum('td,djk->tjk', normed, kv_weight, preferred_element_type=jnp.f...  14.9 us
    scatter x1, other arithmetic, local(): jnp.zeros((adapter_total * capacity, local_width), jnp.bfloat16).at[targets]  11.2 us
    all_gather x1, waiting for transfers between devices, local(): rank_total_sum = jnp.sum(lax.all_gather(down_projected, 'tensor'), axis=0)  9.57 us
    psum x1, blocking collectives, local(): squares = lax.psum(jnp.sum(widened * widened, axis=1), 'tensor')  8.38 us
    all_to_all x1, starting transfers between devices, local(): lax.all_to_all(back_rows, 'store', split_axis=0, concat_axis=0, tiled=True)  5.52 us
  transfers between devices with their start and end apart: 3, of which 3 were waited for; matrix products, arithmetic and copies ran while one was open for 12% of the time, Pallas kernels for 0%

profile of v1, /device:TPU:0, one launch (start us, length us, event | category | flops | bytes accessed | tf_op | source)
XLA Modules:
  0.0 270.2 jit_solution(17537318963463318395)
XLA Ops:
  7.2 1.4 convert_reduce_fusion
  9.4 3.1 %fusion = f32[1024]{0:T(1024)S(1)} fusion(bf16[1024,2048]{1,0:T(8,128)(2,1)} %param.8), kind=kLoop, calls=%fused_computation.4 | loop fusion | flops 6290432 | bytes 4198400 | tf_op jit(solution)/shard_map/reduce_sum | solution.py:70
  12.5 8.4 %psum.7 = f32[1024]{0:T(1024)S(1)} all-reduce(f32[1024]{0:T(1024)S(1)} %fusion), channel_id=1, replica_groups=mesh['store'=8,'tensor'=4] {'tensor'}, use_global_device_ids=true, to_apply=%region_1.0 | all-reduce | flops 1024 | bytes 8192 | tf_op jit(solution)/shard_map/psum | solution.py:70
  20.9 11.2 %scatter_custom_fusion = bf16[1280,2048]{1,0:T(8,128)(2,1)} fusion(s32[1024]{0:T(1024)S(1)} %bitcast.52, bf16[]{:T(256)} %constant.6.clone.1, bf16[1024,2048]{1,0:T(8,128)(2,1)} %param.8, f32[2048]{0:T(1024)S(1)} %copy-done.6, f32[1024]{0:T(1024)S(1)} %add_rsqrt_fusion), kind=kCustom, calls=%fused_computation.15 | custom fusion | flops 8388608 | bytes 9449474 | tf_op jit(solution)/shard_map/scatter | solution.py:76
  32.1 120.3 %all_to_all.10 = bf16[8,4,40,2048]{3,2,1,0:T(8,128)(2,1)S(1)} all-to-all(bf16[8,4,40,2048]{3,2,1,0:T(8,128)(2,1)} %bitcast.47), channel_id=1, replica_groups=mesh['store'=8,'tensor'=4] {'store'}, dimensions={0} | all-to-all | bytes 10485760 | tf_op jit(solution)/shard_map/all_to_all | solution.py:81
  152.4 2.5 fusion.13
  155.2 14.9 %fusion.3 = f32[1024,2,1024]{2,0,1:T(8,128)} fusion(bf16[2048,2,1024]{2,1,0:T(2,128)(2,1)} %param.10, bf16[1024,2048]{1,0:T(8,128)(2,1)} %param.8, f32[2048]{0:T(1024)S(1)} %copy-done.6, f32[1024]{0:T(1024)S(1)} %add_rsqrt_fusion), kind=kOutput, calls=%fused_computation.7 | convolution fusion | flops 8598323200 | bytes 20983808 | tf_op jit(solution)/shard_map/td,djk->tjk/dot_general | solution.py:96
  170.1 9.6 %all-gather.3.cloned.1.call-done = f32[32,4,40,128]{3,2,0,1:T(8,128)} async-done(((f32[8,4,40,128]{3,2,0,1:T(8,128)}), f32[32,4,40,128]{3,2,0,1:T(8,128)}) %all-gather.3.cloned.1.call-update) | async-done | bytes 2621456 | tf_op jit(solution)/shard_map/all_gather | solution.py:85
  179.7 1.9 reduce_sum.48
  182.5 1.3 copy.29
  183.9 1.7 reshape.98
  185.6 5.5 %all-to-all-start.1 = ((bf16[8,4,40,512]{3,2,1,0:T(8,128)(2,1)}), bf16[8,4,40,512]{3,2,1,0:T(8,128)(2,1)S(1)}, u32[]{:S(2)}, u32[]{:S(2)}) async-start(bf16[8,4,40,512]{3,2,1,0:T(8,128)(2,1)} %reshape.98), calls=%async_computation.2 | async-start | bytes 2621440 | tf_op jit(solution)/shard_map/all_to_all | solution.py:94
  191.5 1.9 multiply_cosine_fusion
  193.4 1.3 pad_maximum_fusion
  194.7 28.2 %all-to-all-done.1 = bf16[8,4,40,512]{3,2,1,0:T(8,128)(2,1)S(1)} async-done(((bf16[8,4,40,512]{3,2,1,0:T(8,128)(2,1)}), bf16[8,4,40,512]{3,2,1,0:T(8,128)(2,1)S(1)}, u32[]{:S(2)}, u32[]{:S(2)}) %all-to-all-start.1) | async-done | bytes 1310752 | tf_op jit(solution)/shard_map/all_to_all | solution.py:94
  222.9 1.3 reshape.99
  224.2 5.5 %gather_fusion = bf16[1024,2,256]{2,1,0:T(2,128)(2,1)S(1)} fusion(bf16[1280,2,256]{2,1,0:T(2,128)(2,1)} %reshape.99, s32[1024]{0:T(1024)S(1)} %broadcast_clamp_fusion), kind=kCustom, calls=%fused_computation | custom fusion | bytes 2101248 | tf_op jit(solution)/shard_map/gather | solution.py:95
  229.7 23.8 %reduce-scatter.2.cloned.1.call-done = f32[1024,2,256]{2,0,1:T(8,128)} async-done(((f32[1024,2,1024]{2,0,1:T(8,128)}), f32[1024,2,256]{2,0,1:T(8,128)}) %reduce-scatter.2.cloned.1.call-update) | async-done | bytes 2097168 | tf_op jit(solution)/shard_map/reduce_scatter | solution.py:97
  253.5 1.8 convert_add_fusion
  255.3 1.1 slice.19
  257.8 1.7 reshape_squeeze.6
  259.6 1.1 slice_negate_fusion
  260.8 1.2 maximum_multiply_fusion
  262.4 1.0 fusion.20
  (37 shorter events, 4.1 us)
Async XLA Ops:
  7.2 145.2 %copy-start = (bf16[4,2048,128]{2,1,0:T(8,128)(2,1)S(1)}, bf16[4,2048,128]{2,1,0:T(8,128)(2,1)}, u32[]{:S(2)}) copy-start(bf16[4,2048,128]{2,1,0:T(8,128)(2,1)} %param.11) | copy-start | bytes 6291460
  7.2 13.7 %copy-start.6 = (f32[2048]{0:T(1024)S(1)}, f32[2048]{0:T(1024)}, u32[]{:S(2)}) copy-start(f32[2048]{0:T(1024)} %param.9) | copy-start | bytes 24580
  7.2 172.5 %all-gather.3.cloned.1.call-start = ((), (), s32[]{:S(2)}) async-start(), calls=%async_computation.4 | async-start | bytes 3276800 | tf_op jit(solution)/shard_map/all_gather | solution.py:85
  154.9 98.6 %reduce-scatter.2.cloned.1.call-start = ((), (), s32[]{:S(2)}) async-start(), calls=%async_computation.3 | async-start | bytes 10485760 | tf_op jit(solution)/shard_map/reduce_scatter | solution.py:97
  170.1 11.9 %copy-start.5 = (bf16[4,2,64,256]{3,2,1,0:T(8,128)(2,1)S(1)}, bf16[4,2,64,256]{3,2,1,0:T(8,128)(2,1)}, u32[]{:S(2)}) copy-start(bf16[4,2,64,256]{3,2,1,0:T(8,128)(2,1)} %param.12) | copy-start | bytes 786436
  182.5 8.6 %copy-start.7 = (s32[16]{0:T(128)S(1)}, s32[16]{0:T(128)}, u32[]{:S(2)}) copy-start(s32[16]{0:T(128)} %param.15) | copy-start | bytes 196
  185.6 37.3 %all-to-all-start.1 = ((bf16[8,4,40,512]{3,2,1,0:T(8,128)(2,1)}), bf16[8,4,40,512]{3,2,1,0:T(8,128)(2,1)S(1)}, u32[]{:S(2)}, u32[]{:S(2)}) async-start(bf16[8,4,40,512]{3,2,1,0:T(8,128)(2,1)} %reshape.98), calls=%async_computation.2 | async-start | bytes 2621440 | tf_op jit(solution)/shard_map/all_to_all | solution.py:94
  255.3 1.7 copy-start.1
  259.6 1.2 copy-start.4
  259.6 2.4 copy-start.3
  259.6 2.8 %copy-start.2 = (f32[1024,2,256]{2,0,1:T(8,128)S(1)}, f32[1024,2,256]{2,0,1:T(8,128)}, u32[]{:S(2)}) copy-start(f32[1024,2,256]{2,0,1:T(8,128)} %copy-done.1) | copy-start | bytes 6291460
Sparse Core Ops, SparseCore 0:
  155.1 24.5 all-gather.2
  182.2 71.2 reduce-scatter.1
